TPU v7x, 256 devices: a whole 4x4x8 slice. The times are simulated.
256 devices in a mesh: event: 8 (over x, z_lo), cuts: 32 (over z_hi, y, core).
Axes of the slice: x: 4, y: 4, z: 8 (z_hi: 4, z_lo: 2; z = z_hi * 2 + z_lo), core: 2. Of those that a mesh axis runs over, the one named last changes fastest.
Arguments:
- forward_displacement: float32 [8, 557568], P('event', 'cuts'), may hold values from -6 to 6
- forward_velocity: float32 [8, 557568], P('event', 'cuts'), may hold values from -6 to 6
- adjoint_displacement: float32 [8, 557568], P('event', 'cuts'), may hold values from -6 to 6
- adjoint_velocity: float32 [8, 557568], P('event', 'cuts'), may hold values from -6 to 6
- inverse_mass: float32 [557568], P('cuts'), may hold values from 0.3 to 3
- shear_modulus: float32 [125, 8192], P(None, 'cuts'), may hold values from 0.5 to 4
- connectivity: int32 [125, 8192], P(None, 'cuts'), may hold values from 0 to 18512, as said below
- face_points: int32 [32, 1152], P('cuts'), may hold values from 0 to 1088, as said below
- element_count: int32 [32], P('cuts'), may hold values from 128 to 256, as said below
Outputs:
- forward_displacement_next: float32 [8, 557568], P('event', 'cuts')
- forward_velocity_next: float32 [8, 557568], P('event', 'cuts')
- adjoint_displacement_next: float32 [8, 557568], P('event', 'cuts')
- adjoint_velocity_next: float32 [8, 557568], P('event', 'cuts')
- shear_kernel: float32 [512, 1089], P('cuts')
Inputs may be any that keep to these rules, and one draw needn't show every extreme that they name: `connectivity`: slot n of slice s is the element (ex, ey, ez) of a structured block of 4 x 8 x 8 elements, in an order drawn per slice; its point (i, j, k) has coordinates x = 4 ex + i, y = 4 ey + j, z = 4 ez + k and index x 1089 + y * 33 + z for x < 16; points with x = 16 lie on the next slice's first plane and have index 17424 + g, where g is their slot in the next slice's face list. `face_points`: row s lists in slots 0 to 1088 each point of slice s with x = 0 once; slots 1089 to 1151 hold 0. `element_count`: some slice has all 256 slots live in every draw.
All inputs are finite; a program needn't handle non-finite values.
Results may differ from a plain program's by a relative error of at most 0.0001.
Values sent between devices are 32-bit elements; how exact they have to be, the bound alone decides.
A program may use at most 128 MiB of HBM per device.

v0:
```python
import jax
import jax.numpy as jnp
import numpy as np
from jax import lax
from jax.sharding import PartitionSpec as P

NGLL = 5
PXU = 16
PY = 33
PZ = 33
PYZ = 1089
NPTS = 17424
NBUF = 1152
time_step = 0.02
cross_sigma = 1.5
cross_reach = 4


def from_behind(block, axis, distance):
    devices = range(lax.axis_size(axis))
    route = [((i - distance) % len(devices), i) for i in devices]
    return lax.ppermute(block, axis, route)


def with_halo(cells, sides, width):
    for axis, dim in sides:
        count = lax.axis_size(axis)
        head = lax.slice_in_dim(cells, 0, width, axis=dim)
        tail = lax.slice_in_dim(cells, cells.shape[dim] - width, cells.shape[dim], axis=dim)
        cells = jnp.concatenate(
            [
                lax.ppermute(tail, axis, [(i, (i + 1) % count) for i in range(count)]),
                cells,
                lax.ppermute(head, axis, [((i + 1) % count, i) for i in range(count)]),
            ],
            axis=dim,
        )
    return cells


def gll_tables():
    nodes = np.array([-1.0, -np.sqrt(3.0 / 7.0), 0.0, np.sqrt(3.0 / 7.0), 1.0])
    quad_weights = np.array([0.1, 49.0 / 90.0, 32.0 / 45.0, 49.0 / 90.0, 0.1])
    barycentric = np.array(
        [
            1.0
            / np.prod(
                [
                    nodes[node_row] - nodes[node_column]
                    for node_column in range(5)
                    if node_column != node_row
                ]
            )
            for node_row in range(5)
        ]
    )
    derivative = np.zeros((5, 5))
    for node_row in range(5):
        for node_column in range(5):
            if node_column != node_row:
                derivative[node_row, node_column] = (
                    barycentric[node_column]
                    / barycentric[node_row]
                    / (nodes[node_row] - nodes[node_column])
                )
        derivative[node_row, node_row] = -np.sum(derivative[node_row])
    weights_cube = (
        quad_weights[:, None, None] * quad_weights[None, :, None] * quad_weights[None, None, :]
    ).reshape(125)
    return (
        jnp.asarray(derivative, dtype=jnp.float32),
        jnp.asarray(weights_cube, dtype=jnp.float32),
    )


def gradients(cube, derivative):
    grad_x = jnp.einsum("il,ljkn->ijkn", derivative, cube, precision=lax.Precision.HIGHEST)
    grad_y = jnp.einsum("jl,ilkn->ijkn", derivative, cube, precision=lax.Precision.HIGHEST)
    grad_z = jnp.einsum("kl,ijln->ijkn", derivative, cube, precision=lax.Precision.HIGHEST)
    return (grad_x, grad_y, grad_z)


def stiffness(grads, flux_cube, derivative):
    term_x = jnp.einsum(
        "li,ljkn->ijkn", derivative, flux_cube * grads[0], precision=lax.Precision.HIGHEST
    )
    term_y = jnp.einsum(
        "lj,ilkn->ijkn", derivative, flux_cube * grads[1], precision=lax.Precision.HIGHEST
    )
    term_z = jnp.einsum(
        "lk,ijln->ijkn", derivative, flux_cube * grads[2], precision=lax.Precision.HIGHEST
    )
    return -(term_x + term_y + term_z)


def along_weight(offset):
    sigma = PXU / 4.0
    return jnp.exp(-offset * offset / (2.0 * sigma * sigma))


def along_band():
    offsets = jnp.arange(-PXU, PXU + 1, dtype=jnp.int32).astype(jnp.float32)
    norm_total = jnp.sum(along_weight(offsets))
    row_index = jnp.arange(PXU, dtype=jnp.int32)
    rim_index = jnp.arange(3 * PXU, dtype=jnp.int32)
    spread = rim_index[None, :] - PXU - row_index[:, None]
    inside = (jnp.abs(spread) <= PXU).astype(jnp.float32)
    return along_weight(spread.astype(jnp.float32)) * inside / norm_total


def cross_matrix(count):
    point_index = jnp.arange(count, dtype=jnp.int32)
    offset = (point_index[:, None] - point_index[None, :]).astype(jnp.float32)
    kept = jnp.exp(-offset * offset / (2.0 * cross_sigma * cross_sigma)) * (
        jnp.abs(offset) <= cross_reach
    ).astype(jnp.float32)
    return kept / jnp.sum(kept, axis=1, keepdims=True)


def on_device(
    forward_displacement,
    forward_velocity,
    adjoint_displacement,
    adjoint_velocity,
    inverse_mass,
    shear_modulus,
    connectivity,
    face_points,
    element_count,
):
    derivative, weights_cube = gll_tables()
    faces = face_points[0]
    elements = connectivity.shape[1]
    active = (jnp.arange(elements, dtype=jnp.int32) < element_count[0]).astype(jnp.float32)
    flux = weights_cube[:, None] * shear_modulus * active[None, :]
    flux_cube = flux.reshape(NGLL, NGLL, NGLL, elements)
    forward_now = forward_displacement[0]
    adjoint_now = adjoint_displacement[0]
    both_now = jnp.stack([forward_now, adjoint_now])
    both_ghost = from_behind(both_now[:, faces], "cuts", -1)
    both_ext = jnp.concatenate([both_now, both_ghost], axis=1)
    gathered = both_ext[:, connectivity]
    cubes = gathered.transpose(1, 0, 2).reshape(NGLL, NGLL, NGLL, 2 * elements)
    both_grads = gradients(cubes, derivative)
    both_flux = jnp.concatenate([flux_cube, flux_cube], axis=3)
    both_force = stiffness(both_grads, both_flux, derivative)
    forward_term = both_force[..., :elements]
    adjoint_term = both_force[..., elements:]
    product = (
        both_grads[0][..., :elements] * both_grads[0][..., elements:]
        + both_grads[1][..., :elements] * both_grads[1][..., elements:]
        + both_grads[2][..., :elements] * both_grads[2][..., elements:]
    )
    kernel_term = -flux_cube * product
    stacked_terms = jnp.stack(
        [forward_term.reshape(-1), adjoint_term.reshape(-1), kernel_term.reshape(-1)], axis=1
    )
    point_ids = connectivity.reshape(-1)
    total = NPTS + NBUF
    summed_terms = jax.ops.segment_sum(stacked_terms, point_ids, num_segments=total)
    forward_force = summed_terms[:, 0]
    adjoint_force = summed_terms[:, 1]
    kernel_ext = summed_terms[:, 2]
    back_forward, back_adjoint, back_kernel = from_behind(
        (forward_force[NPTS:], adjoint_force[NPTS:], kernel_ext[NPTS:]), "cuts", 1
    )
    forward_force = forward_force[:NPTS].at[faces].add(back_forward)
    adjoint_force = adjoint_force[:NPTS].at[faces].add(back_adjoint)
    kernel_points = kernel_ext[:NPTS].at[faces].add(back_kernel)
    forward_speed_next = forward_velocity[0] - time_step * inverse_mass * forward_force
    forward_now_next = forward_now - time_step * forward_speed_next
    adjoint_speed_next = adjoint_velocity[0] + time_step * inverse_mass * adjoint_force
    adjoint_now_next = adjoint_now + time_step * adjoint_speed_next
    event_kernel = kernel_points.reshape(PXU, PYZ)
    band = along_band()
    cross = jnp.kron(cross_matrix(PY), cross_matrix(PZ))
    summed = lax.psum(event_kernel, "event")
    rimmed = with_halo(summed, (("cuts", 0),), PXU)
    smoothed_along = jnp.dot(band, rimmed, precision=lax.Precision.HIGHEST)
    shear_kernel = jnp.dot(smoothed_along, cross.T, precision=lax.Precision.HIGHEST)
    return (
        forward_now_next[None, :],
        forward_speed_next[None, :],
        adjoint_now_next[None, :],
        adjoint_speed_next[None, :],
        shear_kernel,
    )


def solution(mesh):
    in_specs = (
        P("event", "cuts"),
        P("event", "cuts"),
        P("event", "cuts"),
        P("event", "cuts"),
        P("cuts"),
        P(None, "cuts"),
        P(None, "cuts"),
        P("cuts", None),
        P("cuts"),
    )
    out_specs = (
        P("event", "cuts"),
        P("event", "cuts"),
        P("event", "cuts"),
        P("event", "cuts"),
        P("cuts", None),
    )
    return jax.shard_map(
        on_device, mesh=mesh, in_specs=in_specs, out_specs=out_specs, check_vma=False
    )
```

profile of v0, /device:TPU:121, one launch (start us, length us, event | category | flops | bytes accessed | tf_op | source)
XLA Modules:
  0.0 436.7 jit_solution(18053370572969491955)
XLA Ops:
  7.2 0.7 fusion.35
  8.0 1.1 pad_maximum_fusion.2
  9.1 5.1 %copy.95 = f32[2,17424]{0,1:T(8,128)} copy(f32[2,17424]{1,0:T(2,128)S(1)} %pad_maximum_fusion.2) | data formatting | bytes 278784 | tf_op jit(solution)/shard_map/stack | solution.py:139
  14.1 6.0 %gather_fusion = f32[1152,2]{1,0:T(8,128)S(1)} fusion(f32[2,17424]{0,1:T(8,128)} %copy.95, s32[2048]{0:T(1024)S(1)} %pad_clamp_fusion.1), kind=kCustom, calls=%fused_computation | custom fusion | bytes 23040 | tf_op jit(solution)/shard_map/gather | solution.py:140
  20.3 0.7 collective-permute-start
  22.1 8.9 %broadcast_multiply_fusion = f32[33,33,33,33]{3,2,1,0:T(8,128)} fusion(f32[33,33]{1,0:T(8,128)S(1)} %fusion.25), kind=kLoop, calls=%fused_computation.6 | loop fusion | flops 1185921 | bytes 4748040 | tf_op jit(solution)/shard_map/jit(kron)/mul | solution.py:176
  31.3 5.3 %copy.97 = f32[2,18576]{0,1:T(8,128)} copy(f32[2,18576]{1,0:T(2,128)S(1)} %pad_maximum_fusion.1) | data formatting | bytes 297216 | tf_op jit(solution)/shard_map/concatenate | solution.py:141
  36.6 63.0 %gather_fusion.1 = f32[32000,2]{1,0:T(8,128)} fusion(f32[2,18576]{0,1:T(8,128)} %copy.97, s32[32768]{0:T(1024)S(1)} %pad_clamp_fusion), kind=kCustom, calls=%fused_computation.1 | custom fusion | bytes 640000 | tf_op jit(solution)/shard_map/gather | solution.py:142
  99.5 9.1 %copy.98 = f32[125,2,256]{2,1,0:T(2,128)S(1)} copy(f32[125,2,256]{1,2,0:T(8,128)} %bitcast.37) | data formatting | bytes 512000 | tf_op jit(solution)/shard_map/transpose | solution.py:143
  111.4 0.6 fusion.4
  112.1 0.6 fusion.6
  112.7 0.8 fusion.3
  114.5 8.5 %copy.114 = f32[32000,3]{1,0:T(8,128)} copy(f32[32000,3]{0,1:T(4,128)S(1)} %pad_maximum_fusion) | data formatting | bytes 768000 | tf_op jit(solution)/shard_map/stack | solution.py:155
  123.0 176.6 %scatter_custom_fusion = f32[18576,3]{1,0:T(8,128)} fusion(s32[32000]{0:T(1024)S(1)} %reshape.155, f32[32000,3]{1,0:T(8,128)} %copy.114, f32[]{:T(128)} %constant.13.clone.1), kind=kCustom, calls=%fused_computation.10 | custom fusion | flops 96000 | bytes 223424 | tf_op jit(solution)/shard_map/scatter-add | solution.py:160
  299.7 2.5 slice_reduce_fusion.3
  302.1 5.4 %collective-permute-start.3 = (f32[1152]{0:T(1024)S(1)}, f32[1152]{0:T(1024)S(1)}, u32[]{:S(2)}, u32[]{:S(2)}) collective-permute-start(f32[1152]{0:T(1024)S(1)} %get-tuple-element.5), channel_id=1, source_target_pairs={{31,0},{0,1},{1,2},{2,3},{3,4},{4,5},{5,6},{6,7},{7,8},{8,9},{9,10... | collective-permute-start | bytes 13832 | tf_op jit(solution)/shard_map/ppermute | solution.py:22
  307.5 16.4 %slice_reduce_fusion = (f32[17424]{0:T(1024)S(1)}, f32[17424]{0:T(1024)S(1)}, f32[17424]{0:T(1024)S(1)}) fusion(f32[18576,3]{1,0:T(8,128)} %scatter_custom_fusion), kind=kLoop, calls=%fused_computation.7 | loop fusion | bytes 418176 | tf_op jit(solution)/shard_map/slice | solution.py:169
  324.1 8.8 %scatter_fusion.2 = f32[17424]{0:T(1024)S(1)} fusion(f32[17424]{0:T(1024)S(1)} %get-tuple-element.8, s32[1152]{0:T(1024)S(1)} %fusion.35, f32[1152]{0:T(1024)S(1)} %collective-permute-done.3), kind=kCustom, calls=%fused_computation.5 | custom fusion | flops 1152 | bytes 18432 | tf_op jit(solution)/shard_map/scatter-add | solution.py:169
  332.9 0.7 reshape.136
  334.1 15.5 %mul.130 = f32[1089,1089]{1,0:T(8,128)} reshape(f32[33,33,33,33]{3,2,1,0:T(8,128)} %broadcast_multiply_fusion) | data formatting | bytes 9487368 | tf_op jit(solution)/shard_map/jit(kron)/mul | solution.py:176
  350.0 0.7 fusion.43
  350.7 8.8 %scatter_fusion = f32[17424]{0:T(1024)S(1)} fusion(f32[17424]{0:T(1024)S(1)} %get-tuple-element.10, s32[1152]{0:T(1024)S(1)} %fusion.35, f32[1152]{0:T(1024)S(1)} %collective-permute-done.1), kind=kCustom, calls=%fused_computation.3 | custom fusion | flops 1152 | bytes 18432 | tf_op jit(solution)/shard_map/scatter-add | solution.py:167
  359.5 9.0 %scatter_fusion.1 = f32[17424]{0:T(1024)S(1)} fusion(f32[17424]{0:T(1024)S(1)} %get-tuple-element.9, s32[1152]{0:T(1024)S(1)} %fusion.35, f32[1152]{0:T(1024)S(1)} %collective-permute-done.2), kind=kCustom, calls=%fused_computation.4 | custom fusion | flops 1152 | bytes 18432 | tf_op jit(solution)/shard_map/scatter-add | solution.py:168
  368.6 35.2 %all-reduce.2.cloned.1.call-done = f32[16,1089]{1,0:T(8,128)} async-done(((f32[16,1089]{1,0:T(8,128)}), f32[16,1089]{1,0:T(8,128)}) %all-reduce.2.cloned.1.call-update) | async-done | bytes 69712 | tf_op jit(solution)/shard_map/psum | solution.py:177
  403.7 8.9 %collective-permute-start.4 = (f32[16,1089]{1,0:T(8,128)}, f32[16,1089]{1,0:T(8,128)S(1)}, u32[]{:S(2)}, u32[]{:S(2)}) collective-permute-start(f32[16,1089]{1,0:T(8,128)} %all-reduce.2.cloned.1.call-done), channel_id=1, source_target_pairs={{0,1},{1,2},{2,3},{3,4},{4,5},{5,6},{6,7},{7,8},{8,9},{9,10},{10,1... | collective-permute-start | bytes 209096 | tf_op jit(solution)/shard_map/ppermute | solution.py:32
  412.6 0.7 broadcast_in_dim.16
  413.3 0.7 broadcast_in_dim.17
  414.0 0.7 broadcast_in_dim.20
  414.7 0.7 broadcast_in_dim.21
  415.4 5.4 %collective-permute-done.5 = f32[16,1089]{1,0:T(8,128)S(1)} collective-permute-done((f32[16,1089]{1,0:T(8,128)}, f32[16,1089]{1,0:T(8,128)S(1)}, u32[]{:S(2)}, u32[]{:S(2)}) %collective-permute-start.5) | collective-permute-done | bytes 69728 | tf_op jit(solution)/shard_map/ppermute | solution.py:34
  420.8 1.8 fusion.13
  422.6 7.3 %fusion.52 = f32[16,1089]{1,0:T(8,128)} fusion(f32[16,1089]{1,0:T(8,128)S(1)} %fusion.13, f32[1089,1089]{1,0:T(8,128)} %mul.130), kind=kOutput, calls=%fused_computation.91 | convolution fusion | flops 227696832 | bytes 4883076 | tf_op jit(solution)/shard_map/dot_general | solution.py:180
  (63 shorter events, 5.4 us)
Async XLA Ops:
  7.2 14.7 %copy-start.8 = (f32[125]{0:T(128)S(1)}, f32[125]{0:T(128)}, u32[]{:S(2)}) copy-start(f32[125]{0:T(128)} %constant.35.clone) | copy-start | bytes 1504
  7.2 14.0 %copy-start.2 = (s32[125,256]{1,0:T(8,128)S(1)}, s32[125,256]{1,0:T(8,128)}, u32[]{:S(2)}) copy-start(s32[125,256]{1,0:T(8,128)} %param.17) | copy-start | bytes 384004
  7.2 14.7 %copy-start.4 = (f32[125,256]{1,0:T(8,128)S(1)}, f32[125,256]{1,0:T(8,128)}, u32[]{:S(2)}) copy-start(f32[125,256]{1,0:T(8,128)} %param.16) | copy-start | bytes 384004
  7.2 396.5 %all-reduce.2.cloned.1.call-start = ((), (), s32[]{:S(2)}) async-start(), calls=%async_computation | async-start | bytes 147456 | tf_op jit(solution)/shard_map/psum | solution.py:177
  20.3 10.8 %collective-permute-start = (f32[2,1152]{1,0:T(2,128)S(1)}, f32[2,1152]{1,0:T(2,128)S(1)}, u32[]{:S(2)}, u32[]{:S(2)}) collective-permute-start(f32[2,1152]{1,0:T(2,128)S(1)} %copy.96), channel_id=1, source_target_pairs={{1,0},{2,1},{3,2},{4,3},{5,4},{6,5},{7,6},{8,7},{9,8},{10,9},{11,1... | collective-permute-start | bytes 27656 | tf_op jit(solution)/shard_map/ppermute | solution.py:22
  22.1 9.0 %copy-start = (f32[1,17424]{1,0:T(1,128)S(1)}, f32[1,17424]{1,0:T(1,128)}, u32[]{:S(2)}) copy-start(f32[1,17424]{1,0:T(1,128)} %param.11) | copy-start | bytes 209092
  22.1 9.0 %copy-start.1 = (f32[1,17424]{1,0:T(1,128)S(1)}, f32[1,17424]{1,0:T(1,128)}, u32[]{:S(2)}) copy-start(f32[1,17424]{1,0:T(1,128)} %param.13) | copy-start | bytes 209092
  36.6 72.3 %copy-start.3 = (f32[5,5,1,1]{1,0,3,2:T(8,128)S(1)}, f32[5,5,1,1]{1,0,3,2:T(8,128)}, u32[]{:S(2)}) copy-start(f32[5,5,1,1]{1,0,3,2:T(8,128)} %constant.43) | copy-start | bytes 304
  302.1 22.0 %collective-permute-start.3 = (f32[1152]{0:T(1024)S(1)}, f32[1152]{0:T(1024)S(1)}, u32[]{:S(2)}, u32[]{:S(2)}) collective-permute-start(f32[1152]{0:T(1024)S(1)} %get-tuple-element.5), channel_id=1, source_target_pairs={{31,0},{0,1},{1,2},{2,3},{3,4},{4,5},{5,6},{6,7},{7,8},{8,9},{9,10... | collective-permute-start | bytes 13832 | tf_op jit(solution)/shard_map/ppermute | solution.py:22
  323.9 26.8 %collective-permute-start.1 = (f32[1152]{0:T(1024)S(1)}, f32[1152]{0:T(1024)S(1)}, u32[]{:S(2)}, u32[]{:S(2)}) collective-permute-start(f32[1152]{0:T(1024)S(1)} %get-tuple-element.7), channel_id=1, source_target_pairs={{31,0},{0,1},{1,2},{2,3},{3,4},{4,5},{5,6},{6,7},{7,8},{8,9},{9,10... | collective-permute-start | bytes 13832 | tf_op jit(solution)/shard_map/ppermute | solution.py:22
  324.0 35.5 %collective-permute-start.2 = (f32[1152]{0:T(1024)S(1)}, f32[1152]{0:T(1024)S(1)}, u32[]{:S(2)}, u32[]{:S(2)}) collective-permute-start(f32[1152]{0:T(1024)S(1)} %get-tuple-element.6), channel_id=1, source_target_pairs={{31,0},{0,1},{1,2},{2,3},{3,4},{4,5},{5,6},{6,7},{7,8},{8,9},{9,10... | collective-permute-start | bytes 13832 | tf_op jit(solution)/shard_map/ppermute | solution.py:22
  334.0 15.6 %copy-start.6 = (f32[1,17424]{1,0:T(1,128)S(1)}, f32[1,17424]{1,0:T(1,128)}, u32[]{:S(2)}) copy-start(f32[1,17424]{1,0:T(1,128)} %param.12) | copy-start | bytes 209092
  334.1 15.7 %copy-start.7 = (f32[1,17424]{1,0:T(1,128)S(1)}, f32[1,17424]{1,0:T(1,128)}, u32[]{:S(2)}) copy-start(f32[1,17424]{1,0:T(1,128)} %param.14) | copy-start | bytes 209092
  359.5 53.1 %copy-start.5 = (f32[17424]{0:T(1024)S(1)}, f32[17424]{0:T(1024)}, u32[]{:S(2)}) copy-start(f32[17424]{0:T(1024)} %param.15) | copy-start | bytes 209092
  403.7 11.7 %collective-permute-start.4 = (f32[16,1089]{1,0:T(8,128)}, f32[16,1089]{1,0:T(8,128)S(1)}, u32[]{:S(2)}, u32[]{:S(2)}) collective-permute-start(f32[16,1089]{1,0:T(8,128)} %all-reduce.2.cloned.1.call-done), channel_id=1, source_target_pairs={{0,1},{1,2},{2,3},{3,4},{4,5},{5,6},{6,7},{7,8},{8,9},{9,10},{10,1... | collective-permute-start | bytes 209096 | tf_op jit(solution)/shard_map/ppermute | solution.py:32
  412.6 8.2 %collective-permute-start.5 = (f32[16,1089]{1,0:T(8,128)}, f32[16,1089]{1,0:T(8,128)S(1)}, u32[]{:S(2)}, u32[]{:S(2)}) collective-permute-start(f32[16,1089]{1,0:T(8,128)} %all-reduce.2.cloned.1.call-done), channel_id=1, source_target_pairs={{1,0},{2,1},{3,2},{4,3},{5,4},{6,5},{7,6},{8,7},{9,8},{10,9},{11,1... | collective-permute-start | bytes 209096 | tf_op jit(solution)/shard_map/ppermute | solution.py:34
Sparse Core Ops, SparseCore 0:
  333.8 69.8 all-reduce.1
where the time goes:
time: 437 us
  other arithmetic  217 us (50%)
  local copies, waits for them, and re-layouts  136 us (31%)
  waiting for transfers between devices  40.6 us (9%)
  starting transfers between devices  15.2 us (3%)
  between operations  15.1 us (3%)
  matrix products  12.8 us (3%)
    scatter-add x1, other arithmetic, on_device(): jax.ops.segment_sum(stacked_terms, point_ids, num_segments=total)  177 us
    gather x1, local copies, waits for them, and re-layouts, on_device(): gathered = both_ext[:, connectivity]  63 us
    psum x1, waiting for transfers between devices, on_device(): summed = lax.psum(event_kernel, 'event')  35.2 us
    slice x1, local copies, waits for them, and re-layouts, on_device(): kernel_points = kernel_ext[:NPTS].at[faces].add(back_kernel)  16.4 us
    mul x1, local copies, waits for them, and re-layouts, on_device(): cross = jnp.kron(cross_matrix(PY), cross_matrix(PZ))  15.5 us
    transpose x1, local copies, waits for them, and re-layouts, on_device(): cubes = gathered.transpose(1, 0, 2).reshape(NGLL, NGLL, NGLL, 2 * elements)  9.08 us
    scatter-add x1, other arithmetic, on_device(): adjoint_force = adjoint_force[:NPTS].at[faces].add(back_adjoint)  9.04 us
    mul x1, other arithmetic, on_device(): cross = jnp.kron(cross_matrix(PY), cross_matrix(PZ))  8.92 us
  transfers between devices with their start and end apart: 7, of which 2 were waited for; matrix products, arithmetic and copies ran while one was open for 17% of the time, Pallas kernels for 0%

commit v1 on v0

--- a/solution.py
+++ b/solution.py
@@ -174,7 +174,8 @@
     event_kernel = kernel_points.reshape(PXU, PYZ)
     band = along_band()
     cross = jnp.kron(cross_matrix(PY), cross_matrix(PZ))
-    summed = lax.psum(event_kernel, "event")
+    parts = lax.all_gather(event_kernel, "event")
+    summed = jnp.sum(parts, axis=0)
     rimmed = with_halo(summed, (("cuts", 0),), PXU)
     smoothed_along = jnp.dot(band, rimmed, precision=lax.Precision.HIGHEST)
     shear_kernel = jnp.dot(smoothed_along, cross.T, precision=lax.Precision.HIGHEST)

time: 437 us -> 410 us (0.938); the launches traced: 437 us -> 403 us
  waiting for transfers between devices: 40.6 us -> 0.02 us
  blocking collectives: 0 us -> 24.5 us
  between operations: 15.1 us -> 1.72 us
    psum x1 -> x0, waiting for transfers between devices: 35.2 us -> none  [on_device(): summed = lax.psum(event_kernel, 'event')]
    all_gather x0 -> x1, blocking collectives: none -> 24.5 us  [on_device(): parts = lax.all_gather(event_kernel, 'event')]
    ppermute x1, waiting for transfers between devices: 5.44 us -> 0.01 us  [with_halo(): lax.ppermute(head, axis, [((i + 1) % count, i) for i in range(count)])]
  transfers between devices with their start and end apart: 7 -> 6, of which waited for: 2 -> 0; matrix products, arithmetic and copies ran while one was open for 17% -> 18% of each run, Pallas kernels for 0% -> 0%
where the time goes in v1:
time: 410 us; the launch traced here: 403 us
  other arithmetic  217 us (53%)
  local copies, waits for them, and re-layouts  135 us (33%)
  blocking collectives  24.5 us (6%)
  starting transfers between devices  12.7 us (3%)
  matrix products  11.9 us (3%)
    scatter-add x1, other arithmetic, on_device(): jax.ops.segment_sum(stacked_terms, point_ids, num_segments=total)  177 us
    gather x1, local copies, waits for them, and re-layouts, on_device(): gathered = both_ext[:, connectivity]  62.8 us
    all_gather x1, blocking collectives, on_device(): parts = lax.all_gather(event_kernel, 'event')  24.5 us
    slice x1, local copies, waits for them, and re-layouts, on_device(): kernel_points = kernel_ext[:NPTS].at[faces].add(back_kernel)  16.4 us
    mul x1, local copies, waits for them, and re-layouts, on_device(): cross = jnp.kron(cross_matrix(PY), cross_matrix(PZ))  15.6 us
    transpose x1, local copies, waits for them, and re-layouts, on_device(): cubes = gathered.transpose(1, 0, 2).reshape(NGLL, NGLL, NGLL, 2 * elements)  9.08 us
    scatter-add x1, other arithmetic, on_device(): adjoint_force = adjoint_force[:NPTS].at[faces].add(back_adjoint)  9.04 us
    mul x1, other arithmetic, on_device(): cross = jnp.kron(cross_matrix(PY), cross_matrix(PZ))  8.92 us
  transfers between devices with their start and end apart: 6, of which 0 were waited for; matrix products, arithmetic and copies ran while one was open for 18% of the time, Pallas kernels for 0%

profile of v1, /device:TPU:121, one launch (start us, length us, event | category | flops | bytes accessed | tf_op | source)
XLA Modules:
  0.0 402.8 jit_solution(6645985841159260579)
XLA Ops:
  0.7 0.8 fusion.35
  1.4 1.1 pad_maximum_fusion.2
  2.5 5.1 %copy.95 = f32[2,17424]{0,1:T(8,128)} copy(f32[2,17424]{1,0:T(2,128)S(1)} %pad_maximum_fusion.2) | data formatting | bytes 278784 | tf_op jit(solution)/shard_map/stack | solution.py:139
  7.5 6.0 %gather_fusion = f32[1152,2]{1,0:T(8,128)S(1)} fusion(f32[2,17424]{0,1:T(8,128)} %copy.95, s32[2048]{0:T(1024)S(1)} %pad_clamp_fusion.1), kind=kCustom, calls=%fused_computation | custom fusion | bytes 23040 | tf_op jit(solution)/shard_map/gather | solution.py:140
  13.7 0.7 collective-permute-start
  15.6 8.9 %broadcast_multiply_fusion = f32[33,33,33,33]{3,2,1,0:T(8,128)} fusion(f32[33,33]{1,0:T(8,128)S(1)} %fusion.25), kind=kLoop, calls=%fused_computation.6 | loop fusion | flops 1185921 | bytes 4748040 | tf_op jit(solution)/shard_map/jit(kron)/mul | solution.py:176
  24.9 15.6 %mul.130 = f32[1089,1089]{1,0:T(8,128)} reshape(f32[33,33,33,33]{3,2,1,0:T(8,128)} %broadcast_multiply_fusion) | data formatting | bytes 9487368 | tf_op jit(solution)/shard_map/jit(kron)/mul | solution.py:176
  40.9 0.6 fusion.43
  41.6 5.3 %copy.97 = f32[2,18576]{0,1:T(8,128)} copy(f32[2,18576]{1,0:T(2,128)S(1)} %pad_maximum_fusion.1) | data formatting | bytes 297216 | tf_op jit(solution)/shard_map/concatenate | solution.py:141
  46.9 62.8 %gather_fusion.1 = f32[32000,2]{1,0:T(8,128)} fusion(f32[2,18576]{0,1:T(8,128)} %copy.97, s32[32768]{0:T(1024)S(1)} %pad_clamp_fusion), kind=kCustom, calls=%fused_computation.1 | custom fusion | bytes 640000 | tf_op jit(solution)/shard_map/gather | solution.py:142
  109.8 9.1 %copy.98 = f32[125,2,256]{2,1,0:T(2,128)S(1)} copy(f32[125,2,256]{1,2,0:T(8,128)} %bitcast.37) | data formatting | bytes 512000 | tf_op jit(solution)/shard_map/transpose | solution.py:143
  119.6 0.6 fusion.8
  120.2 0.6 fusion.10
  121.6 0.6 fusion.4
  122.3 0.6 fusion.6
  122.9 0.8 fusion.3
  124.7 8.4 %copy.114 = f32[32000,3]{1,0:T(8,128)} copy(f32[32000,3]{0,1:T(4,128)S(1)} %pad_maximum_fusion) | data formatting | bytes 768000 | tf_op jit(solution)/shard_map/stack | solution.py:155
  133.2 176.6 %scatter_custom_fusion = f32[18576,3]{1,0:T(8,128)} fusion(s32[32000]{0:T(1024)S(1)} %reshape.151, f32[32000,3]{1,0:T(8,128)} %copy.114, f32[]{:T(128)} %constant.13.clone.1), kind=kCustom, calls=%fused_computation.10 | custom fusion | flops 96000 | bytes 223424 | tf_op jit(solution)/shard_map/scatter-add | solution.py:160
  309.7 2.4 slice_reduce_fusion.3
  312.1 5.4 %collective-permute-start.3 = (f32[1152]{0:T(1024)S(1)}, f32[1152]{0:T(1024)S(1)}, u32[]{:S(2)}, u32[]{:S(2)}) collective-permute-start(f32[1152]{0:T(1024)S(1)} %get-tuple-element.5), channel_id=1, source_target_pairs={{31,0},{0,1},{1,2},{2,3},{3,4},{4,5},{5,6},{6,7},{7,8},{8,9},{9,10... | collective-permute-start | bytes 13832 | tf_op jit(solution)/shard_map/ppermute | solution.py:22
  317.5 16.4 %slice_reduce_fusion = (f32[17424]{0:T(1024)S(1)}, f32[17424]{0:T(1024)S(1)}, f32[17424]{0:T(1024)S(1)}) fusion(f32[18576,3]{1,0:T(8,128)} %scatter_custom_fusion), kind=kLoop, calls=%fused_computation.7 | loop fusion | bytes 418176 | tf_op jit(solution)/shard_map/slice | solution.py:169
  334.1 8.8 %scatter_fusion.2 = f32[17424]{0:T(1024)S(1)} fusion(f32[17424]{0:T(1024)S(1)} %get-tuple-element.8, s32[1152]{0:T(1024)S(1)} %fusion.35, f32[1152]{0:T(1024)S(1)} %collective-permute-done.3), kind=kCustom, calls=%fused_computation.5 | custom fusion | flops 1152 | bytes 18432 | tf_op jit(solution)/shard_map/scatter-add | solution.py:169
  343.1 24.5 %all_gather.3 = f32[8,16,1089]{2,1,0:T(8,128)S(1)} all-gather(f32[1,16,1089]{2,1,0:T(8,128)S(1)} %all_gather_reshape.3), channel_id=1, replica_groups=mesh['event'=8,'cuts'=32] {'event'}, dimensions={0}, use_global_device_ids=true | all-gather | bytes 627264 | tf_op jit(solution)/shard_map/all_gather | solution.py:177
  367.6 6.1 %collective-permute-start.4 = (f32[16,1089]{1,0:T(8,128)S(1)}, f32[16,1089]{1,0:T(8,128)S(1)}, u32[]{:S(2)}, u32[]{:S(2)}) collective-permute-start(f32[16,1089]{1,0:T(8,128)S(1)} %reduce_sum.32), channel_id=1, source_target_pairs={{0,1},{1,2},{2,3},{3,4},{4,5},{5,6},{6,7},{7,8},{8,9},{9,10},{10,1... | collective-permute-start | bytes 209096 | tf_op jit(solution)/shard_map/ppermute | solution.py:32
  374.0 8.8 %scatter_fusion = f32[17424]{0:T(1024)S(1)} fusion(f32[17424]{0:T(1024)S(1)} %get-tuple-element.10, s32[1152]{0:T(1024)S(1)} %fusion.35, f32[1152]{0:T(1024)S(1)} %collective-permute-done.1), kind=kCustom, calls=%fused_computation.3 | custom fusion | flops 1152 | bytes 18432 | tf_op jit(solution)/shard_map/scatter-add | solution.py:167
  382.8 9.0 %scatter_fusion.1 = f32[17424]{0:T(1024)S(1)} fusion(f32[17424]{0:T(1024)S(1)} %get-tuple-element.9, s32[1152]{0:T(1024)S(1)} %fusion.35, f32[1152]{0:T(1024)S(1)} %collective-permute-done.2), kind=kCustom, calls=%fused_computation.4 | custom fusion | flops 1152 | bytes 18432 | tf_op jit(solution)/shard_map/scatter-add | solution.py:168
  391.9 0.7 broadcast_in_dim.16
  392.6 0.7 broadcast_in_dim.17
  393.3 0.7 broadcast_in_dim.20
  394.0 0.7 broadcast_in_dim.21
  394.7 0.9 fusion.13
  395.6 7.3 %fusion.52 = f32[16,1089]{1,0:T(8,128)} fusion(f32[16,1089]{1,0:T(8,128)S(1)} %fusion.13, f32[1089,1089]{1,0:T(8,128)} %mul.130), kind=kOutput, calls=%fused_computation.91 | convolution fusion | flops 227696832 | bytes 4883076 | tf_op jit(solution)/shard_map/dot_general | solution.py:181
  (62 shorter events, 4.6 us)
Async XLA Ops:
  0.6 14.7 %copy-start.8 = (f32[125]{0:T(128)S(1)}, f32[125]{0:T(128)}, u32[]{:S(2)}) copy-start(f32[125]{0:T(128)} %constant.35.clone) | copy-start | bytes 1504
  0.6 13.9 %copy-start.2 = (s32[125,256]{1,0:T(8,128)S(1)}, s32[125,256]{1,0:T(8,128)}, u32[]{:S(2)}) copy-start(s32[125,256]{1,0:T(8,128)} %param.17) | copy-start | bytes 384004
  0.7 14.6 %copy-start.4 = (f32[125,256]{1,0:T(8,128)S(1)}, f32[125,256]{1,0:T(8,128)}, u32[]{:S(2)}) copy-start(f32[125,256]{1,0:T(8,128)} %param.16) | copy-start | bytes 384004
  13.7 27.8 %collective-permute-start = (f32[2,1152]{1,0:T(2,128)S(1)}, f32[2,1152]{1,0:T(2,128)S(1)}, u32[]{:S(2)}, u32[]{:S(2)}) collective-permute-start(f32[2,1152]{1,0:T(2,128)S(1)} %copy.96), channel_id=1, source_target_pairs={{1,0},{2,1},{3,2},{4,3},{5,4},{6,5},{7,6},{8,7},{9,8},{10,9},{11,1... | collective-permute-start | bytes 27656 | tf_op jit(solution)/shard_map/ppermute | solution.py:22
  15.6 9.0 %copy-start.1 = (f32[1,17424]{1,0:T(1,128)S(1)}, f32[1,17424]{1,0:T(1,128)}, u32[]{:S(2)}) copy-start(f32[1,17424]{1,0:T(1,128)} %param.11) | copy-start | bytes 209092
  15.6 9.1 %copy-start = (f32[1,17424]{1,0:T(1,128)S(1)}, f32[1,17424]{1,0:T(1,128)}, u32[]{:S(2)}) copy-start(f32[1,17424]{1,0:T(1,128)} %param.13) | copy-start | bytes 209092
  24.9 15.6 %copy-start.6 = (f32[1,17424]{1,0:T(1,128)S(1)}, f32[1,17424]{1,0:T(1,128)}, u32[]{:S(2)}) copy-start(f32[1,17424]{1,0:T(1,128)} %param.12) | copy-start | bytes 209092
  24.9 15.8 %copy-start.7 = (f32[1,17424]{1,0:T(1,128)S(1)}, f32[1,17424]{1,0:T(1,128)}, u32[]{:S(2)}) copy-start(f32[1,17424]{1,0:T(1,128)} %param.14) | copy-start | bytes 209092
  46.9 72.1 %copy-start.3 = (f32[5,5,1,1]{1,0,3,2:T(8,128)S(1)}, f32[5,5,1,1]{1,0,3,2:T(8,128)}, u32[]{:S(2)}) copy-start(f32[5,5,1,1]{1,0,3,2:T(8,128)} %constant.43) | copy-start | bytes 304
  312.1 22.0 %collective-permute-start.3 = (f32[1152]{0:T(1024)S(1)}, f32[1152]{0:T(1024)S(1)}, u32[]{:S(2)}, u32[]{:S(2)}) collective-permute-start(f32[1152]{0:T(1024)S(1)} %get-tuple-element.5), channel_id=1, source_target_pairs={{31,0},{0,1},{1,2},{2,3},{3,4},{4,5},{5,6},{6,7},{7,8},{8,9},{9,10... | collective-permute-start | bytes 13832 | tf_op jit(solution)/shard_map/ppermute | solution.py:22
  333.9 40.1 %collective-permute-start.1 = (f32[1152]{0:T(1024)S(1)}, f32[1152]{0:T(1024)S(1)}, u32[]{:S(2)}, u32[]{:S(2)}) collective-permute-start(f32[1152]{0:T(1024)S(1)} %get-tuple-element.7), channel_id=1, source_target_pairs={{31,0},{0,1},{1,2},{2,3},{3,4},{4,5},{5,6},{6,7},{7,8},{8,9},{9,10... | collective-permute-start | bytes 13832 | tf_op jit(solution)/shard_map/ppermute | solution.py:22
  334.0 48.8 %collective-permute-start.2 = (f32[1152]{0:T(1024)S(1)}, f32[1152]{0:T(1024)S(1)}, u32[]{:S(2)}, u32[]{:S(2)}) collective-permute-start(f32[1152]{0:T(1024)S(1)} %get-tuple-element.6), channel_id=1, source_target_pairs={{31,0},{0,1},{1,2},{2,3},{3,4},{4,5},{5,6},{6,7},{7,8},{8,9},{9,10... | collective-permute-start | bytes 13832 | tf_op jit(solution)/shard_map/ppermute | solution.py:22
  367.6 27.0 %collective-permute-start.4 = (f32[16,1089]{1,0:T(8,128)S(1)}, f32[16,1089]{1,0:T(8,128)S(1)}, u32[]{:S(2)}, u32[]{:S(2)}) collective-permute-start(f32[16,1089]{1,0:T(8,128)S(1)} %reduce_sum.32), channel_id=1, source_target_pairs={{0,1},{1,2},{2,3},{3,4},{4,5},{5,6},{6,7},{7,8},{8,9},{9,10},{10,1... | collective-permute-start | bytes 209096 | tf_op jit(solution)/shard_map/ppermute | solution.py:32
  373.7 20.9 %collective-permute-start.5 = (f32[16,1089]{1,0:T(8,128)S(1)}, f32[16,1089]{1,0:T(8,128)S(1)}, u32[]{:S(2)}, u32[]{:S(2)}) collective-permute-start(f32[16,1089]{1,0:T(8,128)S(1)} %reduce_sum.32), channel_id=1, source_target_pairs={{1,0},{2,1},{3,2},{4,3},{5,4},{6,5},{7,6},{8,7},{9,8},{10,9},{11,1... | collective-permute-start | bytes 209096 | tf_op jit(solution)/shard_map/ppermute | solution.py:34
  382.8 9.1 %copy-start.5 = (f32[17424]{0:T(1024)S(1)}, f32[17424]{0:T(1024)}, u32[]{:S(2)}) copy-start(f32[17424]{0:T(1024)} %param.15) | copy-start | bytes 209092
